TPU v7x, 32 devices: a whole 2x2x4 slice. The times are simulated.
32 devices in a mesh: rep: 16 (over z, y, core), shard: 2 (over x).
Axes of the slice: x: 2, y: 2, z: 4, core: 2. Of those that a mesh axis runs over, the one named last changes fastest.
Arguments:
- inputs: bfloat16 [4096, 1024], P(('rep', 'shard')), may hold values from -6 to 6
- attn_gain: bfloat16 [1024], P('shard'), may hold values from 0.25 to 1.75
- attn_shift: bfloat16 [1024], P('shard'), may hold values from -3 to 3
- feed_gain: bfloat16 [1024], P('shard'), may hold values from 0.25 to 1.75
- feed_shift: bfloat16 [1024], P('shard'), may hold values from -3 to 3
- qkv_weight: bfloat16 [1024, 3072], P(None, 'shard'), may hold values from -0.1875 to 0.1875
- qkv_bias: bfloat16 [3072], P('shard'), may hold values from -3 to 3
- out_weight: bfloat16 [1024, 1024], P(None, 'shard'), may hold values from -0.75 to 0.75
- out_bias: bfloat16 [1024], P('shard'), may hold values from -3 to 3
- up_weight: bfloat16 [1024, 4096], P(None, 'shard'), may hold values from -0.1875 to 0.1875
- up_bias: bfloat16 [4096], P('shard'), may hold values from -3 to 3
- down_weight: bfloat16 [4096, 1024], P('shard'), may hold values from -0.09375 to 0.09375
- down_bias: bfloat16 [1024], P('shard'), may hold values from -3 to 3
- cotangent: bfloat16 [4096, 1024], P(('rep', 'shard')), may hold values from -6 to 6
Outputs:
- outputs: bfloat16 [4096, 1024], P(('rep', 'shard'))
- input_grad: float32 [4096, 1024], P(('rep', 'shard'))
- grad_attn_gain: float32 [1024], P('shard')
- grad_attn_shift: float32 [1024], P('shard')
- grad_feed_gain: float32 [1024], P('shard')
- grad_feed_shift: float32 [1024], P('shard')
- grad_qkv_weight: float32 [1024, 3072], P(None, 'shard')
- grad_qkv_bias: float32 [3072], P('shard')
- grad_out_weight: float32 [1024, 1024], P(None, 'shard')
- grad_out_bias: float32 [1024], P('shard')
- grad_up_weight: float32 [1024, 4096], P(None, 'shard')
- grad_up_bias: float32 [4096], P('shard')
- grad_down_weight: float32 [4096, 1024], P('shard')
- grad_down_bias: float32 [1024], P('shard')
All inputs are finite; a program needn't handle non-finite values.
Results may differ from a plain program's by a relative error of at most 0.012.
Values may be sent and summed in bfloat16 or wider, within the bound.
No kernel may reach another device: no remote copies, remote signals or barrier semaphores. Data moves between devices by JAX's collectives and lax.ppermute only.
A program may use at most 192 MiB of HBM per device.

v0:
```python
import math

import jax
import jax.numpy as jnp
from jax import lax
from jax.sharding import PartitionSpec as P

D = 1024
H = 16
HD = 64
ROT = 16


norm_eps = 1e-05
base_freq = 10000.0


def rotary_tables(length, rotary_dims):
    half_dims = rotary_dims // 2
    positions = jnp.arange(length).astype(jnp.float32)
    inverse = jnp.exp(
        jnp.arange(half_dims).astype(jnp.float32) * (-2.0 * math.log(base_freq) / rotary_dims)
    )
    angles = positions[:, None] * inverse[None, :]
    return (jnp.cos(angles), jnp.sin(angles))


def rotate(values, cosine, sine_table, rotary_dims, direction):
    half_dims = rotary_dims // 2
    lower_half = values[..., :half_dims]
    upper_half = values[..., half_dims:rotary_dims]
    cosine_row = cosine[:, None, :]
    sine_row = sine_table[:, None, :] * direction
    return jnp.concatenate(
        [
            lower_half * cosine_row - upper_half * sine_row,
            upper_half * cosine_row + lower_half * sine_row,
            values[..., rotary_dims:],
        ],
        axis=-1,
    )


def gelu_slope(preact):
    normal_cdf = 0.5 * (1.0 + jax.scipy.special.erf(preact * (1.0 / math.sqrt(2.0))))
    return normal_cdf + preact * jnp.exp(-0.5 * preact * preact) * (1.0 / math.sqrt(2.0 * math.pi))


def body(
    inputs,
    attn_gain,
    attn_shift,
    feed_gain,
    feed_shift,
    qkv_weight,
    qkv_bias,
    out_weight,
    out_bias,
    up_weight,
    up_bias,
    down_weight,
    down_bias,
    cotangent,
):
    (
        gain_one,
        shift_one,
        gain_two,
        shift_two,
        out_bias_all,
        down_bias_all,
        qkv_all,
        qkv_bias_all,
        out_all,
    ) = (
        lax.all_gather(attn_gain, "shard", axis=0, tiled=True),
        lax.all_gather(attn_shift, "shard", axis=0, tiled=True),
        lax.all_gather(feed_gain, "shard", axis=0, tiled=True),
        lax.all_gather(feed_shift, "shard", axis=0, tiled=True),
        lax.all_gather(out_bias, "shard", axis=0, tiled=True),
        lax.all_gather(down_bias, "shard", axis=0, tiled=True),
        lax.all_gather(qkv_weight, "shard", axis=1, tiled=True),
        lax.all_gather(qkv_bias, "shard", axis=0, tiled=True),
        lax.all_gather(out_weight, "shard", axis=1, tiled=True),
    )
    gain_one = gain_one.astype(jnp.float32)
    gain_two = gain_two.astype(jnp.float32)
    length = inputs.shape[0]
    resid = inputs.astype(jnp.float32)
    row_mean = jnp.mean(resid, -1, keepdims=True)
    centered = resid - row_mean
    inv_std = lax.rsqrt(jnp.mean(centered * centered, -1, keepdims=True) + norm_eps)
    normed = centered * inv_std
    attn_in = (normed * gain_one + shift_one.astype(jnp.float32)).astype(jnp.bfloat16)
    feed_in = (normed * gain_two + shift_two.astype(jnp.float32)).astype(jnp.bfloat16)
    projected = jnp.dot(attn_in, qkv_all, preferred_element_type=jnp.float32) + qkv_bias_all.astype(
        jnp.float32
    )
    projected = projected.reshape(length, 3, H, HD)
    cosine, sine_table = rotary_tables(length, ROT)
    query_rot = rotate(projected[:, 0], cosine, sine_table, ROT, 1.0).astype(jnp.bfloat16)
    keys_rot = rotate(projected[:, 1], cosine, sine_table, ROT, 1.0).astype(jnp.bfloat16)
    values_b = projected[:, 2].astype(jnp.bfloat16)
    score_scale = 1.0 / math.sqrt(HD)
    row_block = min(512, length)
    block_count = length // row_block
    key_positions = jnp.arange(length)

    def block_scores(row_start, q_rows):
        scores = (
            jnp.einsum("qhd,khd->hqk", q_rows, keys_rot, preferred_element_type=jnp.float32)
            * score_scale
        )
        causal = (row_start + jnp.arange(row_block))[:, None] >= key_positions[None, :]
        return jnp.where(causal[None], scores, -jnp.inf)

    def forward_block(block_index):
        row_start = block_index * row_block
        scores = block_scores(row_start, query_rot)
        row_max = jnp.max(scores, -1, keepdims=True)
        log_total = row_max + jnp.log(jnp.sum(jnp.exp(scores - row_max), -1, keepdims=True))
        attn_probs = jnp.exp(scores - log_total).astype(jnp.bfloat16)
        block_out = jnp.einsum(
            "hqk,khd->qhd", attn_probs, values_b, preferred_element_type=jnp.float32
        )
        return (block_out.astype(jnp.bfloat16), log_total)

    attended, log_totals = lax.map(forward_block, jnp.arange(block_count))
    attended = attended.reshape(length, D)
    attn_out = jnp.dot(attended, out_all, preferred_element_type=jnp.float32) + out_bias_all.astype(
        jnp.float32
    )
    group_in = lax.all_gather(feed_in, "shard", axis=0, tiled=True)
    preact = jnp.dot(group_in, up_weight, preferred_element_type=jnp.float32) + up_bias.astype(
        jnp.float32
    )
    hidden = jax.nn.gelu(preact, approximate=False).astype(jnp.bfloat16)
    rows_in = hidden
    feed_out = lax.psum_scatter(
        jnp.dot(rows_in, down_weight, preferred_element_type=jnp.float32),
        "shard",
        scatter_dimension=0,
        tiled=True,
    ) + down_bias_all.astype(jnp.float32)
    outputs = (resid + attn_out + feed_out).astype(jnp.bfloat16)
    grad_top = cotangent.astype(jnp.float32)
    attn_group, attended_group, out_back = (
        lax.all_gather(attn_in, "shard", axis=0, tiled=True),
        lax.all_gather(attended, "shard", axis=0, tiled=True),
        lax.all_gather(out_weight, "shard", axis=1, tiled=True),
    )
    grad_cols = lax.all_to_all(cotangent, "shard", split_axis=1, concat_axis=0, tiled=True)
    grad_bias = jnp.sum(grad_cols.astype(jnp.float32), 0)
    grad_out_w = jnp.dot(attended_group.T, grad_cols, preferred_element_type=jnp.float32)
    grad_attended = (
        jnp.dot(cotangent, out_back.T, preferred_element_type=jnp.float32)
        .astype(jnp.bfloat16)
        .reshape(length, H, HD)
    )
    group_grad = lax.all_gather(cotangent, "shard", axis=0, tiled=True)
    grad_down = jnp.dot(hidden.T, group_grad, preferred_element_type=jnp.float32)
    grad_preact = jnp.dot(
        group_grad, down_weight.T, preferred_element_type=jnp.float32
    ) * gelu_slope(preact)
    grad_up_b = jnp.sum(grad_preact, 0)
    grad_preact_b = grad_preact.astype(jnp.bfloat16)
    grad_up = jnp.dot(group_in.T, grad_preact_b, preferred_element_type=jnp.float32)
    rows_in = grad_preact_b
    grad_feed_in = lax.psum_scatter(
        jnp.dot(rows_in, up_weight.T, preferred_element_type=jnp.float32),
        "shard",
        scatter_dimension=0,
        tiled=True,
    )

    def backward_block(carry, block_index):
        grad_keys, grad_values = carry
        row_start = block_index * row_block
        scores = block_scores(row_start, query_rot)
        probs_f = jnp.exp(scores - log_totals[block_index])
        probs_b = probs_f.astype(jnp.bfloat16)
        grad_values = grad_values + jnp.einsum(
            "hqk,qhd->khd", probs_b, grad_attended, preferred_element_type=jnp.float32
        )
        grad_probs = jnp.einsum(
            "qhd,khd->hqk", grad_attended, values_b, preferred_element_type=jnp.float32
        )
        grad_scores = (
            probs_f * (grad_probs - jnp.sum(probs_f * grad_probs, -1, keepdims=True)) * score_scale
        )
        grad_scores_b = grad_scores.astype(jnp.bfloat16)
        grad_qrot = jnp.einsum(
            "hqk,khd->qhd", grad_scores_b, keys_rot, preferred_element_type=jnp.float32
        )
        grad_keys = grad_keys + jnp.einsum(
            "hqk,qhd->khd", grad_scores_b, query_rot, preferred_element_type=jnp.float32
        )
        return ((grad_keys, grad_values), grad_qrot)

    empty_heads = jnp.zeros((length, H, HD), jnp.float32)
    (grad_krot, grad_values), grad_qrot = lax.scan(
        backward_block, (empty_heads, empty_heads), jnp.arange(block_count)
    )
    grad_qrot = grad_qrot.reshape(length, H, HD)
    grad_query = rotate(grad_qrot, cosine, sine_table, ROT, -1.0)
    grad_keys = rotate(grad_krot, cosine, sine_table, ROT, -1.0)
    grad_proj = jnp.stack([grad_query, grad_keys, grad_values], axis=1).reshape(length, 3 * D)
    grad_qkv_b = jnp.sum(grad_proj, 0)
    grad_proj_b = grad_proj.astype(jnp.bfloat16)
    proj_cols = lax.all_to_all(grad_proj_b, "shard", split_axis=1, concat_axis=0, tiled=True)
    grad_qkv = jnp.dot(attn_group.T, proj_cols, preferred_element_type=jnp.float32)
    rows_in = proj_cols
    grad_attn_in = lax.psum_scatter(
        jnp.dot(rows_in, qkv_weight.T, preferred_element_type=jnp.float32),
        "shard",
        scatter_dimension=0,
        tiled=True,
    )
    grad_gain_one = jnp.sum(grad_attn_in * normed, 0)
    grad_shift_one = jnp.sum(grad_attn_in, 0)
    grad_gain_two = jnp.sum(grad_feed_in * normed, 0)
    grad_shift_two = jnp.sum(grad_feed_in, 0)
    grad_normed = grad_attn_in * gain_one + grad_feed_in * gain_two
    input_grad = grad_top + inv_std * (
        grad_normed
        - jnp.mean(grad_normed, -1, keepdims=True)
        - normed * jnp.mean(grad_normed * normed, -1, keepdims=True)
    )
    grad_qkv_b, grad_gain_one, grad_shift_one, grad_gain_two, grad_shift_two = (
        lax.psum_scatter(grad_qkv_b, "shard", scatter_dimension=0, tiled=True),
        lax.psum_scatter(grad_gain_one, "shard", scatter_dimension=0, tiled=True),
        lax.psum_scatter(grad_shift_one, "shard", scatter_dimension=0, tiled=True),
        lax.psum_scatter(grad_gain_two, "shard", scatter_dimension=0, tiled=True),
        lax.psum_scatter(grad_shift_two, "shard", scatter_dimension=0, tiled=True),
    )
    (
        grad_gain_one,
        grad_shift_one,
        grad_gain_two,
        grad_shift_two,
        grad_qkv,
        grad_qkv_b,
        grad_out_w,
        grad_bias,
        grad_up,
        grad_up_b,
        grad_down,
    ) = lax.psum(
        (
            grad_gain_one,
            grad_shift_one,
            grad_gain_two,
            grad_shift_two,
            grad_qkv,
            grad_qkv_b,
            grad_out_w,
            grad_bias,
            grad_up,
            grad_up_b,
            grad_down,
        ),
        "rep",
    )
    return (
        outputs,
        input_grad,
        grad_gain_one,
        grad_shift_one,
        grad_gain_two,
        grad_shift_two,
        grad_qkv,
        grad_qkv_b,
        grad_out_w,
        grad_bias,
        grad_up,
        grad_up_b,
        grad_down,
        grad_bias,
    )


def solution(mesh):
    return jax.shard_map(
        body,
        mesh=mesh,
        in_specs=(
            P(("rep", "shard"), None),
            P("shard"),
            P("shard"),
            P("shard"),
            P("shard"),
            P(None, "shard"),
            P("shard"),
            P(None, "shard"),
            P("shard"),
            P(None, "shard"),
            P("shard"),
            P("shard", None),
            P("shard"),
            P(("rep", "shard"), None),
        ),
        out_specs=(
            P(("rep", "shard"), None),
            P(("rep", "shard"), None),
            P("shard"),
            P("shard"),
            P("shard"),
            P("shard"),
            P(None, "shard"),
            P("shard"),
            P(None, "shard"),
            P("shard"),
            P(None, "shard"),
            P("shard"),
            P("shard", None),
            P("shard"),
        ),
        check_vma=False,
    )
```

profile of v0, /device:TPU:0, one launch (start us, length us, event | category | flops | bytes accessed | tf_op | source)
XLA Modules:
  0.0 687.4 jit_solution(4346178672658685678)
XLA Ops:
  8.8 5.3 all-gather.5
  14.1 4.4 all-gather.4
  18.5 4.4 all-gather.1
  22.9 4.6 all-gather
  28.2 13.8 %all_gather.48 = bf16[256,1024]{1,0:T(8,128)(2,1)S(1)} all-gather(bf16[128,1024]{1,0:T(8,128)(2,1)S(1)} %get-tuple-element.103), channel_id=1, replica_groups=mesh['rep'=16,'shard'=2] {'shard'}, dimensions={0}, use_global_device_ids=true | all-gather | bytes 786432 | tf_op jit(solution)/shard_map/all_gather | solution.py:133
  41.9 7.7 %fusion.3 = (bf16[256,2048]{1,0:T(8,128)(2,1)S(1)}, f32[256,2048]{1,0:T(8,128)S(1)}) fusion(f32[2048]{0:T(1024)S(1)} %convert_element_type.171, bf16[256,1024]{1,0:T(8,128)(2,1)S(1)} %all_gather.48, bf16[1024,2048]{1,0:T(8,128)(2,1)} %param.23), kind=kOutput, calls=%fused_computation.8 | convolution fusion | flops 1108344832 | bytes 7872512 | tf_op jit(solution)/shard_map/dot_general | solution.py:134
  50.6 2.3 fusion.77
  53.0 7.0 %all_gather.50 = bf16[256,1024]{1,0:T(8,128)(2,1)S(1)} all-gather(bf16[128,1024]{1,0:T(8,128)(2,1)S(1)} %copy-done.6), channel_id=1, replica_groups=mesh['rep'=16,'shard'=2] {'shard'}, dimensions={0}, use_global_device_ids=true | all-gather | bytes 786432 | tf_op jit(solution)/shard_map/all_gather | solution.py:160
  60.0 5.6 fusion.76
  66.6 2.3 fusion.51
  69.0 4.8 all-gather.2
  73.9 2.4 convolution_convert_fusion
  77.2 56.0 %all-gather.10.cloned.1.call-done = bf16[1024,3072]{1,0:T(8,128)(2,1)} async-done(((bf16[1024,1536]{1,0:T(8,128)(2,1)}), bf16[1024,3072]{1,0:T(8,128)(2,1)}) %all-gather.10.cloned.1.call-update) | async-done | bytes 6291472 | tf_op jit(solution)/shard_map/all_gather | solution.py:82
  133.2 3.8 convolution_add_fusion
  138.4 1.3 fusion.62
  140.5 3.1 convolution_bitcast_fusion.2
  143.7 1.0 slice.74
  144.7 3.0 convolution_bitcast_fusion.1
  147.6 1.1 slice.77
  150.6 1.0 fusion.24
  151.6 2.3 copy.59
  153.9 4.3 all-to-all-start
  158.2 1.8 copy.60
  160.0 13.6 %all-to-all-done = bf16[128,2,1536]{2,0,1:T(8,128)(2,1)} async-done(((bf16[128,2,1536]{2,0,1:T(8,128)(2,1)}), bf16[128,2,1536]{2,0,1:T(8,128)(2,1)}, u32[]{:S(2)}, u32[]{:S(2)}) %all-to-all-start) | async-done | bytes 786464 | tf_op jit(solution)/shard_map/all_to_all | solution.py:210
  173.6 4.1 all-to-all-start.1
  177.8 4.2 fusion.78
  182.1 6.2 fusion.49
  188.3 4.7 fusion.81
  193.0 13.3 %all_gather.51 = bf16[256,1024]{1,0:T(8,128)(2,1)} all-gather(bf16[128,1024]{1,0:T(8,128)(2,1)S(1)} %copy-done.9), channel_id=1, replica_groups=mesh['rep'=16,'shard'=2] {'shard'}, dimensions={0}, use_global_device_ids=true | all-gather | bytes 786432 | tf_op jit(solution)/shard_map/all_gather | solution.py:148
  206.3 1.8 copy.61
  209.1 7.4 %all_gather.52 = bf16[256,1024]{0,1:T(8,128)(2,1)S(1)} all-gather(bf16[128,1024]{0,1:T(8,128)(2,1)S(1)} %bitcast.75), channel_id=1, replica_groups=mesh['rep'=16,'shard'=2] {'shard'}, dimensions={0}, use_global_device_ids=true | all-gather | bytes 786432 | tf_op jit(solution)/shard_map/all_gather | solution.py:149
  216.5 1.8 fusion.80
  218.3 4.9 fusion.79
  223.8 4.5 all-gather.6
  228.3 4.4 all-gather.3
  234.6 1.1 convert_reduce_fusion.1
  235.7 1.5 fusion.23
  237.3 2.4 fusion.22
  239.7 1.6 fusion.72
  241.4 8.8 %all-reduce.7 = (f32[1024]{0:T(1024)S(1)}, f32[1024]{0:T(1024)S(1)}, f32[1024]{0:T(1024)S(1)}, f32[1024]{0:T(1024)S(1)}, f32[3072]{0:T(1024)S(1)}) all-reduce(f32[1024]{0:T(1024)S(1)} %get-tuple-element.93, f32[1024]{0:T(1024)S(1)} %get-tuple-element.94, ...), channel_id=5, replica_groups=mesh['rep'=16,'shard'=2] {'shard'}, use_global_device_ids=true, to_apply=%region_11.12.clone | all-reduce | flops 7168 | bytes 57344
  250.5 61.1 %all-reduce.5 = (f32[512]{0:T(512)}, f32[512]{0:T(512)}, f32[512]{0:T(512)}, f32[512]{0:T(512)}, f32[1536]{0:T(1024)}, /*index=5*/f32[512]{0:T(512)S(1)}, f32[2048]{0:T(1024)}) all-reduce(f32[512]{0:T(512)S(1)} %dynamic-slice.2, f32[512]{0:T(512)S(1)} %dynamic-slice.4, ...), channel_id=1, replica_groups=mesh['rep'=16,'shard'=2] {'rep'}, use_global_device_ids=true, to_apply=%region_12.13 | all-reduce | flops 6144 | bytes 49152 | tf_op jit(solution)/shard_map/psum | solution.py:248
  311.7 1.0 fusion.45
  312.7 349.5 %all-reduce.10.cloned.1.call-done = (f32[1024,1536]{1,0:T(8,128)}, f32[1024,512]{1,0:T(8,128)}, f32[1024,2048]{1,0:T(8,128)}, f32[2048,1024]{1,0:T(8,128)}) async-done(((f32[1024,1536]{1,0:T(8,128)}, f32[1024,512]{1,0:T(8,128)}, f32[1024,2048]{1,0:T(8,128)}, f32[2048,1024]{1,0:T(8,128)}), (f32[1024,1536]{1,0:T(8,128)}, f32[1024,512]{1,0:T(8,128)}, f32[1024,2048]{1,0:T(8,128)}, ...) | async-done | bytes 25165840 | tf_op jit(solution)/shard_map/psum | solution.py:248
  662.7 6.6 copy.72
  669.3 1.3 copy.73
  671.6 4.3 copy.74
  675.9 1.3 slice-done.1
  677.2 3.4 copy.75
  (140 shorter events, 13.7 us)
Async XLA Ops:
  7.2 1.6 copy-start.27
  7.2 6.9 %copy-start.28 = (bf16[512]{0:T(512)(128)(2,1)S(1)}, bf16[512]{0:T(512)(128)(2,1)}, u32[]{:S(2)}) copy-start(bf16[512]{0:T(512)(128)(2,1)} %param.17) | copy-start | bytes 3076
  7.2 11.3 %copy-start.29 = (bf16[512]{0:T(512)(128)(2,1)S(1)}, bf16[512]{0:T(512)(128)(2,1)}, u32[]{:S(2)}) copy-start(bf16[512]{0:T(512)(128)(2,1)} %param.16) | copy-start | bytes 3076
  7.2 15.7 %copy-start.30 = (bf16[512]{0:T(512)(128)(2,1)S(1)}, bf16[512]{0:T(512)(128)(2,1)}, u32[]{:S(2)}) copy-start(bf16[512]{0:T(512)(128)(2,1)} %param.15) | copy-start | bytes 3076
  7.2 20.3 %copy-start.24 = (bf16[2048]{0:T(1024)(128)(2,1)S(1)}, bf16[2048]{0:T(1024)(128)(2,1)}, u32[]{:S(2)}) copy-start(bf16[2048]{0:T(1024)(128)(2,1)} %param.24) | copy-start | bytes 12292
  7.2 20.3 %copy-start = (bf16[128,1024]{1,0:T(8,128)(2,1)S(1)}, bf16[128,1024]{1,0:T(8,128)(2,1)}, u32[]{:S(2)}) copy-start(bf16[128,1024]{1,0:T(8,128)(2,1)} %param.14) | copy-start | bytes 786436
  7.2 66.7 %all-gather.12.cloned.1.call-start = ((), (), s32[]{:S(2)}) async-start(), calls=%async_computation.6 | async-start | bytes 3145728 | tf_op jit(solution)/shard_map/all_gather | solution.py:84
  8.0 125.2 %all-gather.10.cloned.1.call-start = ((), (), s32[]{:S(2)}) async-start(), calls=%async_computation.5 | async-start | bytes 9437184 | tf_op jit(solution)/shard_map/all_gather | solution.py:82
  8.7 228.6 %reduce-scatter.4.cloned.1.call-start = ((), (), s32[]{:S(2)}) async-start(), calls=%async_computation.7 | async-start | bytes 1572864 | tf_op jit(solution)/shard_map/reduce_scatter | solution.py:139
  28.2 105.0 %copy-start.8 = (bf16[128,1024]{1,0:T(8,128)(2,1)}, bf16[128,1024]{1,0:T(8,128)(2,1)S(1)}, u32[]{:S(2)}) copy-start(bf16[128,1024]{1,0:T(8,128)(2,1)S(1)} %get-tuple-element.104) | copy-start | bytes 786436
  41.9 7.7 %copy-start.14 = (bf16[256,1024]{1,0:T(8,128)(2,1)}, bf16[256,1024]{1,0:T(8,128)(2,1)S(1)}, u32[]{:S(2)}) copy-start(bf16[256,1024]{1,0:T(8,128)(2,1)S(1)} %all_gather.48) | copy-start | bytes 1572868
  41.9 8.6 %copy-start.33 = (bf16[2048,1024]{1,0:T(8,128)(2,1)S(1)}, bf16[2048,1024]{1,0:T(8,128)(2,1)}, u32[]{:S(2)}) copy-start(bf16[2048,1024]{1,0:T(8,128)(2,1)} %param.25) | copy-start | bytes 12582916
  49.6 1.0 copy-start.18
  50.6 2.4 copy-start.6
  52.9 186.8 %reduce-scatter.8.cloned.1.call-start = ((), (), s32[]{:S(2)}) async-start(), calls=%async_computation.9 | async-start | bytes 1572864 | tf_op jit(solution)/shard_map/reduce_scatter | solution.py:169
  60.0 5.6 copy-start.15
  60.0 6.6 copy-start.34
  65.6 1.0 copy-start.20
  66.6 2.3 copy-start.25
  137.4 1.0 copy-start.11
  139.8 0.6 copy-start.22
  147.6 2.2 copy-start.12
  149.8 0.8 copy-start.5
  149.8 1.8 copy-start.3
  153.9 19.7 %all-to-all-start = ((bf16[128,2,1536]{2,0,1:T(8,128)(2,1)}), bf16[128,2,1536]{2,0,1:T(8,128)(2,1)}, u32[]{:S(2)}, u32[]{:S(2)}) async-start(bf16[128,2,1536]{2,0,1:T(8,128)(2,1)} %copy.59), calls=%async_computation.1 | async-start | bytes 1572864 | tf_op jit(solution)/shard_map/all_to_all | solution.py:210
  173.6 32.7 %all-to-all-start.1 = ((bf16[128,2,512]{0,2,1:T(8,128)(2,1)}), bf16[128,2,512]{0,2,1:T(8,128)(2,1)}, u32[]{:S(2)}, u32[]{:S(2)}) async-start(bf16[128,2,512]{0,2,1:T(8,128)(2,1)} %bitcast.77), calls=%async_computation.4 | async-start | bytes 524288 | tf_op jit(solution)/shard_map/all_to_all | solution.py:152
  177.7 62.0 %reduce-scatter.6.cloned.1.call-start = ((), (), s32[]{:S(2)}) async-start(), calls=%async_computation.8 | async-start | bytes 1572864 | tf_op jit(solution)/shard_map/reduce_scatter | solution.py:213
  182.0 480.1 %all-reduce.10.cloned.1.call-start = ((), (), s32[]{:S(2)}) async-start(), calls=%async_computation.10 | async-start | bytes 50331648 | tf_op jit(solution)/shard_map/psum | solution.py:248
  182.1 6.2 copy-start.16
  182.1 6.2 copy-start.19
  188.3 4.7 copy-start.9
  208.1 8.4 %copy-start.21 = (bf16[2,128,512]{2,1,0:T(8,128)(2,1)S(1)}, bf16[2,128,512]{2,1,0:T(8,128)(2,1)}, u32[]{:S(2)}) copy-start(bf16[2,128,512]{2,1,0:T(8,128)(2,1)} %copy.61) | copy-start | bytes 786436
  208.4 0.7 copy-start.13
  208.4 9.9 %copy-start.10 = (bf16[256,1024]{1,0:T(8,128)(2,1)S(1)}, bf16[256,1024]{1,0:T(8,128)(2,1)}, u32[]{:S(2)}) copy-start(bf16[256,1024]{1,0:T(8,128)(2,1)} %all_gather.51) | copy-start | bytes 1572868
  223.1 0.7 copy-start.31
  223.1 5.2 copy-start.32
  223.2 9.6 %copy-start.35 = (u32[32]{0:T(128)S(1)}, u32[32]{0:T(128)}, u32[]{:S(2)}) copy-start(u32[32]{0:T(128)} %constant.123) | copy-start | bytes 388
  223.2 12.6 %copy-start.4 = (f32[128,1,16,64]{0,3,2,1:T(8,128)S(1)}, f32[128,1,16,64]{0,3,2,1:T(8,128)}, u32[]{:S(2)}) copy-start(f32[128,1,16,64]{0,3,2,1:T(8,128)} %copy-done.3) | copy-start | bytes 1572868
  223.2 14.2 %copy-start.2 = (bf16[1024,1024]{1,0:T(8,128)(2,1)S(1)}, bf16[1024,1024]{1,0:T(8,128)(2,1)}, u32[]{:S(2)}) copy-start(bf16[1024,1024]{1,0:T(8,128)(2,1)} %all-gather.12.cloned.1.call-done) | copy-start | bytes 6291460
  237.3 13.2 %copy-start.23 = (f32[2048]{0:T(1024)S(1)}, f32[2048]{0:T(1024)}, u32[]{:S(2)}) copy-start(f32[2048]{0:T(1024)} %get-tuple-element.116) | copy-start | bytes 24580
  237.3 74.3 %copy-start.7 = (bf16[128,1024]{1,0:T(8,128)(2,1)S(1)}, bf16[128,1024]{1,0:T(8,128)(2,1)}, u32[]{:S(2)}) copy-start(bf16[128,1024]{1,0:T(8,128)(2,1)} %param.27) | copy-start | bytes 786436
  311.6 357.7 %copy-start.26 = (f32[512]{0:T(512)}, f32[512]{0:T(512)S(1)}, u32[]{:S(2)}) copy-start(f32[512]{0:T(512)S(1)} %get-tuple-element.159) | copy-start | bytes 6148
  662.7 6.6 copy-start.17
  662.7 8.9 %copy-start.1 = (f32[1024,2048]{1,0:T(8,128)S(1)}, f32[1024,2048]{1,0:T(8,128)}, u32[]{:S(2)}) copy-start(f32[1024,2048]{1,0:T(8,128)} %get-tuple-element.160) | copy-start | bytes 25165828
  669.3 6.5 slice-start
  671.6 5.6 slice-start.1
Sparse Core Ops, SparseCore 0:
  9.6 41.4 all-gather.11
  52.7 80.4 all-gather.9
  135.4 20.3 reduce-scatter.3
  157.9 24.9 reduce-scatter.7
  185.1 25.8 reduce-scatter.5
  223.3 438.7 all-reduce.9
where the time goes:
time: 688 us; the launch traced here: 687 us
  waiting for transfers between devices  420 us (61%)
  blocking collectives  144 us (21%)
  matrix products  56.7 us (8%)
  local copies, waits for them, and re-layouts  33.6 us (5%)
  between operations  15.9 us (2%)
  starting transfers between devices  8.66 us (1%)
  other arithmetic  8.42 us (1%)
    psum x1, waiting for transfers between devices, body(): lax.psum((grad_gain_one, grad_shift_one, grad_gain_two, grad_shift_two, g...  349 us
    psum x1, blocking collectives, body(): lax.psum((grad_gain_one, grad_shift_one, grad_gain_two, grad_shift_two, g...  61.1 us
    all_gather x1, waiting for transfers between devices, body(): lax.all_gather(qkv_weight, 'shard', axis=1, tiled=True)  56 us
    unnamed x95, local copies, waits for them, and re-layouts  25.9 us
  transfers between devices with their start and end apart: 8, of which 3 were waited for; matrix products, arithmetic and copies ran while one was open for 11% of the time, Pallas kernels for 0%

commit v1 on v0

--- a/solution.py
+++ b/solution.py
@@ -233,34 +233,18 @@
         lax.psum_scatter(grad_gain_two, "shard", scatter_dimension=0, tiled=True),
         lax.psum_scatter(grad_shift_two, "shard", scatter_dimension=0, tiled=True),
     )
-    (
-        grad_gain_one,
-        grad_shift_one,
-        grad_gain_two,
-        grad_shift_two,
-        grad_qkv,
-        grad_qkv_b,
-        grad_out_w,
-        grad_bias,
-        grad_up,
-        grad_up_b,
-        grad_down,
-    ) = lax.psum(
-        (
-            grad_gain_one,
-            grad_shift_one,
-            grad_gain_two,
-            grad_shift_two,
-            grad_qkv,
-            grad_qkv_b,
-            grad_out_w,
-            grad_bias,
-            grad_up,
-            grad_up_b,
-            grad_down,
-        ),
-        "rep",
-    )
+    grad_qkv, grad_out_w, grad_up, grad_down = [
+        lax.psum(g.astype(jnp.bfloat16), "rep").astype(jnp.float32)
+        for g in (grad_qkv, grad_out_w, grad_up, grad_down)
+    ]
+    vectors = (grad_gain_one, grad_shift_one, grad_gain_two, grad_shift_two, grad_qkv_b, grad_bias, grad_up_b)
+    summed = lax.psum(jnp.concatenate(vectors), "rep")
+    cuts = []
+    start = 0
+    for vector in vectors:
+        cuts.append(summed[start : start + vector.shape[0]])
+        start += vector.shape[0]
+    grad_gain_one, grad_shift_one, grad_gain_two, grad_shift_two, grad_qkv_b, grad_bias, grad_up_b = cuts
     return (
         outputs,
         input_grad,

time: 688 us -> 476 us (0.69)
  waiting for transfers between devices: 420 us -> 200 us
  blocking collectives: 144 us -> 161 us
  other arithmetic: 8.42 us -> 24.5 us
  local copies, waits for them, and re-layouts: 33.6 us -> 18.4 us
    psum x1, waiting for transfers between devices: 349 us -> 143 us  [body(): lax.psum(g.astype(jnp.bfloat16), 'rep').astype(jnp.float32)]
    all_to_all x0 -> x1, blocking collectives: none -> 17.3 us  [body(): lax.all_to_all(grad_proj_b, 'shard', split_axis=1, concat_axis=0, tiled=T...]
    unnamed x95 -> x94, local copies, waits for them, and re-layouts: 25.9 us -> 8.98 us
    convert_element_type x0 -> x4, other arithmetic: none -> 16.1 us  [body(): lax.psum(g.astype(jnp.bfloat16), 'rep').astype(jnp.float32)]
    all_to_all x1 -> x0, waiting for transfers between devices: 13.6 us -> none  [body(): lax.all_to_all(grad_proj_b, 'shard', split_axis=1, concat_axis=0, tiled=T...]
  transfers between devices with their start and end apart: 8 -> 7, of which waited for: 3 -> 2; matrix products, arithmetic and copies ran while one was open for 11% -> 15% of each run, Pallas kernels for 0% -> 0%
where the time goes in v1:
time: 476 us; the launch traced here: 475 us
  waiting for transfers between devices  200 us (42%)
  blocking collectives  161 us (34%)
  matrix products  50.7 us (11%)
  other arithmetic  24.5 us (5%)
  local copies, waits for them, and re-layouts  18.4 us (4%)
  between operations  15.9 us (3%)
    psum x1, waiting for transfers between devices, body(): lax.psum(g.astype(jnp.bfloat16), 'rep').astype(jnp.float32)  143 us
    psum x1, blocking collectives, body(): summed = lax.psum(jnp.concatenate(vectors), 'rep')  61.2 us
    all_gather x1, waiting for transfers between devices, body(): lax.all_gather(qkv_weight, 'shard', axis=1, tiled=True)  56 us
    all_to_all x1, blocking collectives, body(): lax.all_to_all(grad_proj_b, 'shard', split_axis=1, concat_axis=0, tiled=T...  17.3 us
    convert_element_type x4, other arithmetic, body(): lax.psum(g.astype(jnp.bfloat16), 'rep').astype(jnp.float32)  16.1 us
    all_gather x1, blocking collectives, body(): group_in = lax.all_gather(feed_in, 'shard', axis=0, tiled=True)  13.8 us
    all_gather x1, blocking collectives, body(): lax.all_gather(attn_in, 'shard', axis=0, tiled=True)  13.3 us
  transfers between devices with their start and end apart: 7, of which 2 were waited for; matrix products, arithmetic and copies ran while one was open for 15% of the time, Pallas kernels for 0%

profile of v1, /device:TPU:0, one launch (start us, length us, event | category | flops | bytes accessed | tf_op | source)
XLA Modules:
  0.0 475.4 jit_solution(3831998343974649100)
XLA Ops:
  8.8 5.3 %all-gather.5 = bf16[2,1,512]{2,1,0:T(2,128)(2,1)S(1)} all-gather(bf16[1,1,512]{2,1,0:T(2,128)(2,1)S(1)} %reshape.202), channel_id=1, replica_groups=mesh['rep'=16,'shard'=2] {'shard'}, dimensions={0}, use_global_device_ids=true | all-gather | bytes 3072 | tf_op jit(solution)/shard_map/all_gather | solution.py:79
  14.1 4.4 all-gather.4
  18.5 4.4 all-gather.1
  22.9 4.6 all-gather
  28.2 13.8 %all_gather.48 = bf16[256,1024]{1,0:T(8,128)(2,1)S(1)} all-gather(bf16[128,1024]{1,0:T(8,128)(2,1)S(1)} %get-tuple-element.96), channel_id=1, replica_groups=mesh['rep'=16,'shard'=2] {'shard'}, dimensions={0}, use_global_device_ids=true | all-gather | bytes 786432 | tf_op jit(solution)/shard_map/all_gather | solution.py:133
  41.9 7.7 %fusion.3 = (bf16[256,2048]{1,0:T(8,128)(2,1)S(1)}, f32[256,2048]{1,0:T(8,128)S(1)}) fusion(f32[2048]{0:T(1024)S(1)} %convert_element_type.195, bf16[256,1024]{1,0:T(8,128)(2,1)S(1)} %all_gather.48, bf16[1024,2048]{1,0:T(8,128)(2,1)} %param.23), kind=kOutput, calls=%fused_computation.11 | convolution fusion | flops 1108344832 | bytes 7872512 | tf_op jit(solution)/shard_map/dot_general | solution.py:134
  50.6 2.2 fusion.77
  52.9 7.0 %all_gather.50 = bf16[256,1024]{1,0:T(8,128)(2,1)S(1)} all-gather(bf16[128,1024]{1,0:T(8,128)(2,1)S(1)} %copy-done.7), channel_id=1, replica_groups=mesh['rep'=16,'shard'=2] {'shard'}, dimensions={0}, use_global_device_ids=true | all-gather | bytes 786432 | tf_op jit(solution)/shard_map/all_gather | solution.py:160
  60.0 5.6 %fusion.76 = (f32[2048]{0:T(1024)}, bf16[256,2048]{1,0:T(8,128)(2,1)S(1)}) fusion(f32[256,2048]{1,0:T(8,128)S(1)} %get-tuple-element.113, bf16[256,1024]{1,0:T(8,128)(2,1)S(1)} %all_gather.50, bf16[2048,1024]{1,0:T(8,128)(2,1)} %param.25), kind=kOutput, calls=%fused_computation.135 | convolution fusion | flops 1079506944 | bytes 7872512 | tf_op jit(solution)/shard_map/dot_general | solution.py:162
  65.6 1.0 copy-done.24
  66.6 2.3 fusion.50
  69.0 4.8 %all-gather.2 = bf16[2,1,1536]{2,1,0:T(2,128)(2,1)S(1)} all-gather(bf16[1,1,1536]{2,1,0:T(2,128)(2,1)S(1)} %reshape.196), channel_id=1, replica_groups=mesh['rep'=16,'shard'=2] {'shard'}, dimensions={0}, use_global_device_ids=true | all-gather | bytes 9216 | tf_op jit(solution)/shard_map/all_gather | solution.py:83
  73.9 2.4 convolution_convert_fusion.4
  77.2 56.0 %all-gather.10.cloned.1.call-done = bf16[1024,3072]{1,0:T(8,128)(2,1)} async-done(((bf16[1024,1536]{1,0:T(8,128)(2,1)}), bf16[1024,3072]{1,0:T(8,128)(2,1)}) %all-gather.10.cloned.1.call-update) | async-done | bytes 6291472 | tf_op jit(solution)/shard_map/all_gather | solution.py:82
  133.2 3.8 convolution_add_fusion
  138.4 1.3 fusion.61
  140.6 2.9 convolution_bitcast_fusion.2
  143.5 1.0 slice.102
  144.5 2.9 convolution_bitcast_fusion.1
  147.4 1.1 slice.105
  148.5 1.0 multiply_subtract_fusion.1
  150.4 1.0 fusion.24
  151.4 2.3 copy.59
  153.7 17.3 %all_to_all.35 = bf16[128,2,1536]{2,0,1:T(8,128)(2,1)S(1)} all-to-all(bf16[128,2,1536]{2,0,1:T(8,128)(2,1)} %copy.59), channel_id=1, replica_groups=mesh['rep'=16,'shard'=2] {'shard'}, dimensions={1} | all-to-all | bytes 1572864 | tf_op jit(solution)/shard_map/all_to_all | solution.py:210
  171.9 3.9 fusion.78
  175.8 1.8 copy.60
  177.6 4.1 all-to-all-start.1
  181.8 4.8 %convolution_convert_fusion.2 = bf16[1024,2048]{1,0:T(8,128)(2,1)} fusion(bf16[256,1024]{1,0:T(8,128)(2,1)} %copy-done.12, bf16[256,2048]{1,0:T(8,128)(2,1)} %copy-done.24), kind=kOutput, calls=%fused_computation.3 | convolution fusion | flops 1075838976 | bytes 5767168 | tf_op jit(solution)/shard_map/dot_general | solution.py:167
  186.6 3.3 convolution_convert_fusion.1
  189.9 13.3 %all_gather.51 = bf16[256,1024]{1,0:T(8,128)(2,1)} all-gather(bf16[128,1024]{1,0:T(8,128)(2,1)S(1)} %copy-done.10), channel_id=1, replica_groups=mesh['rep'=16,'shard'=2] {'shard'}, dimensions={0}, use_global_device_ids=true | all-gather | bytes 786432 | tf_op jit(solution)/shard_map/all_gather | solution.py:148
  203.2 1.8 copy.61
  206.0 7.6 %all_gather.52 = bf16[256,1024]{0,1:T(8,128)(2,1)S(1)} all-gather(bf16[128,1024]{0,1:T(8,128)(2,1)S(1)} %bitcast.75), channel_id=1, replica_groups=mesh['rep'=16,'shard'=2] {'shard'}, dimensions={0}, use_global_device_ids=true | all-gather | bytes 786432 | tf_op jit(solution)/shard_map/all_gather | solution.py:149
  213.6 1.4 convolution_convert_fusion.3
  215.0 2.7 convolution_convert_fusion
  218.4 4.5 all-gather.6
  222.9 4.4 all-gather.3
  229.1 1.1 convert_reduce_fusion.1
  230.3 1.5 fusion.23
  231.9 2.4 fusion.22
  234.3 1.6 fusion.71
  235.9 8.8 %all-reduce.5 = (f32[1024]{0:T(1024)S(1)}, f32[1024]{0:T(1024)S(1)}, f32[1024]{0:T(1024)S(1)}, f32[1024]{0:T(1024)S(1)}, f32[3072]{0:T(1024)S(1)}) all-reduce(f32[1024]{0:T(1024)S(1)} %get-tuple-element.86, f32[1024]{0:T(1024)S(1)} %get-tuple-element.87, ...), channel_id=5, replica_groups=mesh['rep'=16,'shard'=2] {'shard'}, use_global_device_ids=true, to_apply=%region_11.12.clone | all-reduce | flops 7168 | bytes 57344
  245.1 61.2 %psum.35 = f32[6144]{0:T(1024)S(1)} all-reduce(f32[6144]{0:T(1024)S(1)} %constant_dynamic-update-slice_fusion), channel_id=1, replica_groups=mesh['rep'=16,'shard'=2] {'rep'}, use_global_device_ids=true, to_apply=%region_22.23 | all-reduce | flops 6144 | bytes 49152 | tf_op jit(solution)/shard_map/psum | solution.py:241
  308.2 1.0 fusion.45
  309.2 142.6 %all-reduce.9.cloned.1.call-done = (bf16[1024,1536]{1,0:T(8,128)(2,1)}, bf16[1024,512]{1,0:T(8,128)(2,1)}, bf16[1024,2048]{1,0:T(8,128)(2,1)}, bf16[2048,1024]{1,0:T(8,128)(2,1)}) async-done(((bf16[1024,1536]{1,0:T(8,128)(2,1)}, bf16[1024,512]{1,0:T(8,128)(2,1)}, bf16[1024,2048]{1,0:T(8,128)(2,1)}, bf16[2048,1024]{1,0:T(8,128)(2,1)}), (bf16[1024,1536]{1,0:T(8,128)(2,1)}, bf16[1024,512]{1,0:T(8,128)(2,1)}, ...) | async-done | bytes 12582928 | tf_op jit(solution)/shard_map/psum | solution.py:237
  451.8 5.6 %convert_element_type.207 = f32[1024,1536]{1,0:T(8,128)} convert(bf16[1024,1536]{1,0:T(8,128)(2,1)} %get-tuple-element.76) | non-fusion elementwise | flops 1572864 | bytes 9437184 | tf_op jit(solution)/shard_map/convert_element_type | solution.py:237
  457.5 1.6 convert_element_type.209
  459.1 4.4 convert_element_type.211
  463.5 4.4 convert_element_type.213
  (146 shorter events, 13.5 us)
Async XLA Ops:
  7.2 1.6 copy-start.30
  7.2 6.9 %copy-start.31 = (bf16[512]{0:T(512)(128)(2,1)S(1)}, bf16[512]{0:T(512)(128)(2,1)}, u32[]{:S(2)}) copy-start(bf16[512]{0:T(512)(128)(2,1)} %param.17) | copy-start | bytes 3076
  7.2 11.3 %copy-start.32 = (bf16[512]{0:T(512)(128)(2,1)S(1)}, bf16[512]{0:T(512)(128)(2,1)}, u32[]{:S(2)}) copy-start(bf16[512]{0:T(512)(128)(2,1)} %param.16) | copy-start | bytes 3076
  7.2 15.7 %copy-start.33 = (bf16[512]{0:T(512)(128)(2,1)S(1)}, bf16[512]{0:T(512)(128)(2,1)}, u32[]{:S(2)}) copy-start(bf16[512]{0:T(512)(128)(2,1)} %param.15) | copy-start | bytes 3076
  7.2 20.3 %copy-start.28 = (bf16[2048]{0:T(1024)(128)(2,1)S(1)}, bf16[2048]{0:T(1024)(128)(2,1)}, u32[]{:S(2)}) copy-start(bf16[2048]{0:T(1024)(128)(2,1)} %param.24) | copy-start | bytes 12292
  7.2 20.3 %copy-start = (bf16[128,1024]{1,0:T(8,128)(2,1)S(1)}, bf16[128,1024]{1,0:T(8,128)(2,1)}, u32[]{:S(2)}) copy-start(bf16[128,1024]{1,0:T(8,128)(2,1)} %param.14) | copy-start | bytes 786436
  7.2 66.7 %all-gather.12.cloned.1.call-start = ((), (), s32[]{:S(2)}) async-start(), calls=%async_computation.6 | async-start | bytes 3145728 | tf_op jit(solution)/shard_map/all_gather | solution.py:84
  8.0 125.2 %all-gather.10.cloned.1.call-start = ((), (), s32[]{:S(2)}) async-start(), calls=%async_computation.5 | async-start | bytes 9437184 | tf_op jit(solution)/shard_map/all_gather | solution.py:82
  8.7 223.1 %reduce-scatter.4.cloned.1.call-start = ((), (), s32[]{:S(2)}) async-start(), calls=%async_computation.7 | async-start | bytes 1572864 | tf_op jit(solution)/shard_map/reduce_scatter | solution.py:139
  28.2 105.0 %copy-start.9 = (bf16[128,1024]{1,0:T(8,128)(2,1)}, bf16[128,1024]{1,0:T(8,128)(2,1)S(1)}, u32[]{:S(2)}) copy-start(bf16[128,1024]{1,0:T(8,128)(2,1)S(1)} %get-tuple-element.97) | copy-start | bytes 786436
  41.9 7.7 %copy-start.12 = (bf16[256,1024]{1,0:T(8,128)(2,1)}, bf16[256,1024]{1,0:T(8,128)(2,1)S(1)}, u32[]{:S(2)}) copy-start(bf16[256,1024]{1,0:T(8,128)(2,1)S(1)} %all_gather.48) | copy-start | bytes 1572868
  41.9 8.6 %copy-start.36 = (bf16[2048,1024]{1,0:T(8,128)(2,1)S(1)}, bf16[2048,1024]{1,0:T(8,128)(2,1)}, u32[]{:S(2)}) copy-start(bf16[2048,1024]{1,0:T(8,128)(2,1)} %param.25) | copy-start | bytes 12582916
  49.6 1.0 copy-start.15
  50.6 2.3 copy-start.7
  52.9 181.4 %reduce-scatter.8.cloned.1.call-start = ((), (), s32[]{:S(2)}) async-start(), calls=%async_computation.9 | async-start | bytes 1572864 | tf_op jit(solution)/shard_map/reduce_scatter | solution.py:169
  60.0 5.6 %copy-start.20 = (bf16[256,1024]{1,0:T(8,128)(2,1)}, bf16[256,1024]{1,0:T(8,128)(2,1)S(1)}, u32[]{:S(2)}) copy-start(bf16[256,1024]{1,0:T(8,128)(2,1)S(1)} %all_gather.50) | copy-start | bytes 1572868
  60.0 6.6 %copy-start.37 = (bf16[1024,2048]{1,0:T(8,128)(2,1)S(1)}, bf16[1024,2048]{1,0:T(8,128)(2,1)}, u32[]{:S(2)}) copy-start(bf16[1024,2048]{1,0:T(8,128)(2,1)} %param.23) | copy-start | bytes 12582916
  65.6 1.0 copy-start.24
  66.6 2.4 copy-start.29
  68.8 165.4 %reduce-scatter.6.cloned.1.call-start = ((), (), s32[]{:S(2)}) async-start(), calls=%async_computation.8 | async-start | bytes 1572864 | tf_op jit(solution)/shard_map/reduce_scatter | solution.py:213
  137.4 1.0 copy-start.17
  139.8 0.6 copy-start.25
  147.4 2.2 copy-start.18
  149.6 0.8 copy-start.4
  149.6 1.8 copy-start.2
  171.0 0.9 copy-start.13
  177.6 25.6 %all-to-all-start.1 = ((bf16[128,2,512]{0,2,1:T(8,128)(2,1)}), bf16[128,2,512]{0,2,1:T(8,128)(2,1)}, u32[]{:S(2)}, u32[]{:S(2)}) async-start(bf16[128,2,512]{0,2,1:T(8,128)(2,1)} %bitcast.78), calls=%async_computation.4 | async-start | bytes 524288 | tf_op jit(solution)/shard_map/all_to_all | solution.py:152
  181.7 270.1 %all-reduce.9.cloned.1.call-start = ((), (), s32[]{:S(2)}) async-start(), calls=%async_computation.10 | async-start | bytes 25165824 | tf_op jit(solution)/shard_map/psum | solution.py:237
  181.7 4.8 %copy-start.16 = (bf16[256,2048]{1,0:T(8,128)(2,1)S(1)}, bf16[256,2048]{1,0:T(8,128)(2,1)}, u32[]{:S(2)}) copy-start(bf16[256,2048]{1,0:T(8,128)(2,1)} %copy-done.15) | copy-start | bytes 3145732
  181.8 4.8 %copy-start.21 = (bf16[256,1024]{1,0:T(8,128)(2,1)S(1)}, bf16[256,1024]{1,0:T(8,128)(2,1)}, u32[]{:S(2)}) copy-start(bf16[256,1024]{1,0:T(8,128)(2,1)} %copy-done.20) | copy-start | bytes 1572868
  186.6 3.3 copy-start.10
  205.0 8.6 %copy-start.23 = (bf16[2,128,512]{2,1,0:T(8,128)(2,1)S(1)}, bf16[2,128,512]{2,1,0:T(8,128)(2,1)}, u32[]{:S(2)}) copy-start(bf16[2,128,512]{2,1,0:T(8,128)(2,1)} %copy.61) | copy-start | bytes 786436
  205.0 10.0 %copy-start.11 = (bf16[256,1024]{1,0:T(8,128)(2,1)S(1)}, bf16[256,1024]{1,0:T(8,128)(2,1)}, u32[]{:S(2)}) copy-start(bf16[256,1024]{1,0:T(8,128)(2,1)} %all_gather.51) | copy-start | bytes 1572868
  205.0 10.0 %copy-start.14 = (bf16[128,2,1536]{2,0,1:T(8,128)(2,1)S(1)}, bf16[128,2,1536]{2,0,1:T(8,128)(2,1)}, u32[]{:S(2)}) copy-start(bf16[128,2,1536]{2,0,1:T(8,128)(2,1)} %copy-done.13) | copy-start | bytes 2359300
  205.3 0.7 copy-start.19
  217.7 0.7 copy-start.34
  217.7 5.2 %copy-start.35 = (bf16[512]{0:T(512)(128)(2,1)S(1)}, bf16[512]{0:T(512)(128)(2,1)}, u32[]{:S(2)}) copy-start(bf16[512]{0:T(512)(128)(2,1)} %param.22) | copy-start | bytes 3076
  217.7 9.6 %copy-start.38 = (u32[32]{0:T(128)S(1)}, u32[32]{0:T(128)}, u32[]{:S(2)}) copy-start(u32[32]{0:T(128)} %constant.123) | copy-start | bytes 388
  217.7 12.6 %copy-start.3 = (f32[128,1,16,64]{0,3,2,1:T(8,128)S(1)}, f32[128,1,16,64]{0,3,2,1:T(8,128)}, u32[]{:S(2)}) copy-start(f32[128,1,16,64]{0,3,2,1:T(8,128)} %copy-done.2) | copy-start | bytes 1572868
  217.7 14.2 %copy-start.1 = (bf16[1024,1024]{1,0:T(8,128)(2,1)S(1)}, bf16[1024,1024]{1,0:T(8,128)(2,1)}, u32[]{:S(2)}) copy-start(bf16[1024,1024]{1,0:T(8,128)(2,1)} %all-gather.12.cloned.1.call-done) | copy-start | bytes 6291460
  231.9 13.3 %copy-start.27 = (f32[2048]{0:T(1024)S(1)}, f32[2048]{0:T(1024)}, u32[]{:S(2)}) copy-start(f32[2048]{0:T(1024)} %get-tuple-element.114) | copy-start | bytes 24580
  231.9 76.3 %copy-start.8 = (bf16[128,1024]{1,0:T(8,128)(2,1)S(1)}, bf16[128,1024]{1,0:T(8,128)(2,1)}, u32[]{:S(2)}) copy-start(bf16[128,1024]{1,0:T(8,128)(2,1)} %param.27) | copy-start | bytes 786436
  308.1 159.8 %copy-start.26 = (f32[512]{0:T(512)}, f32[512]{0:T(512)S(1)}, u32[]{:S(2)}) copy-start(f32[512]{0:T(512)S(1)} %get-tuple-element.147) | copy-start | bytes 6148
  451.8 5.6 %copy-start.22 = (bf16[1024,512]{1,0:T(8,128)(2,1)S(1)}, bf16[1024,512]{1,0:T(8,128)(2,1)}, u32[]{:S(2)}) copy-start(bf16[1024,512]{1,0:T(8,128)(2,1)} %get-tuple-element.77) | copy-start | bytes 3145732
  451.8 7.2 %copy-start.6 = (bf16[1024,2048]{1,0:T(8,128)(2,1)S(1)}, bf16[1024,2048]{1,0:T(8,128)(2,1)}, u32[]{:S(2)}) copy-start(bf16[1024,2048]{1,0:T(8,128)(2,1)} %get-tuple-element.78) | copy-start | bytes 12582916
  459.1 4.5 copy-start.5
Sparse Core Ops, SparseCore 0:
  9.6 41.4 all-gather.11
  52.7 80.4 all-gather.9
  136.0 20.3 reduce-scatter.3
  158.5 22.0 reduce-scatter.7
  182.7 25.4 reduce-scatter.5
  217.9 233.9 all-reduce.8
